TPU v7x, 32 devices: a whole 2x2x4 slice. The times are simulated.
32 devices in a mesh: row: 16 (over z, y, x), col: 2 (over core).
Axes of the slice: x: 2, y: 2, z: 4, core: 2. Of those that a mesh axis runs over, the one named last changes fastest.
Arguments:
- acts: bfloat16 [2048, 8192], P('row'), may hold values from -22 to 22
- out_grads: bfloat16 [2048, 4096], P('row', 'col'), may hold values from -0.198873782 to 0.198873782
- weight: float32 [8192, 4096], P('row', 'col'), may hold values from -30 to 30
- row_state: float32 [8192], P('row'), may hold values from 0.002 to 2
- col_state: float32 [4096], P('col'), may hold values from 0.01 to 0.3
Outputs:
- new_weight: float32 [8192, 4096], P('row', 'col')
- update: float32 [8192, 4096], P('row', 'col')
- row_moment: float32 [8192], P('row')
- col_moment: float32 [4096], P('col')
All inputs are finite; a program needn't handle non-finite values.
Results may differ from a plain program's by a relative error of at most 0.0003.
Values may be sent and summed in bfloat16 or wider, within the bound.
No kernel may reach another device: no remote copies, remote signals or barrier semaphores. Data moves between devices by JAX's collectives and lax.ppermute only.
A program may use at most 64 MiB of HBM per device.

v0:
```python
import jax
import jax.numpy as jnp
from jax import lax
from jax.sharding import PartitionSpec as P

decay_rate = 0.85
floor_eps = 1e-30
relative_rate = 0.05


def per_device(acts, out_grads, weight, row_state, col_state):
    n_col = lax.axis_size("col")
    width = acts.shape[1]
    cols_here = out_grads.shape[1]
    cols_all = cols_here * n_col
    columns = lax.all_to_all(acts, "row", split_axis=1, concat_axis=0, tiled=True)
    gradient = lax.dot_general(
        columns,
        lax.all_gather(out_grads, "row", axis=0, tiled=True),
        (((0,), (0,)), ((), ())),
        preferred_element_type=jnp.float32,
    )
    squares = gradient * gradient + floor_eps
    row_squares = jnp.sum(squares, axis=1)
    col_squares = jnp.sum(squares, axis=0)
    weight_part = jnp.sum(weight * weight)
    row_total = lax.psum(row_squares, "col")
    col_total = lax.psum(col_squares, "row")
    weight_total = lax.psum(weight_part, ("row", "col"))
    row_moment = decay_rate * row_state + (1.0 - decay_rate) * (row_total / cols_all)
    col_moment = decay_rate * col_state + (1.0 - decay_rate) * (col_total / width)
    unclipped = gradient * lax.rsqrt(row_moment[:, None] * col_moment[None, :])
    update_total = lax.psum(jnp.sum(unclipped * unclipped), ("row", "col"))
    count_all = width * cols_all
    clip_factor = jnp.maximum(1.0, jnp.sqrt(update_total / count_all))
    update = unclipped / clip_factor
    step_size = relative_rate * jnp.sqrt(weight_total / count_all + 1e-06)
    new_weight = weight - step_size * update
    return (new_weight, update, row_moment, col_moment)


def solution(mesh):
    return jax.shard_map(
        per_device,
        mesh=mesh,
        in_specs=(P("row", None), P("row", "col"), P("row", "col"), P("row"), P("col")),
        out_specs=(P("row", "col"), P("row", "col"), P("row"), P("col")),
        check_vma=False,
    )
```

profile of v0, /device:TPU:12, one launch (start us, length us, event | category | flops | bytes accessed | tf_op | source)
XLA Modules:
  0.0 269.7 jit_solution(2994545322753481755)
XLA Ops:
  7.2 0.0 all-gather.2.cloned.1.call-start
  7.2 0.7 all-gather.2.cloned.1.call-update
  7.9 4.1 %copy.9 = bf16[128,8192]{0,1:T(8,128)(2,1)} copy(bf16[128,8192]{1,0:T(8,128)(2,1)} %param.5) | data formatting | bytes 4194304 | tf_op args[0]
  12.0 7.2 %all-to-all-start = ((bf16[128,16,512]{0,2,1:T(8,128)(2,1)}), bf16[128,16,512]{0,2,1:T(8,128)(2,1)S(1)}, u32[]{:S(2)}, u32[]{:S(2)}) async-start(bf16[128,16,512]{0,2,1:T(8,128)(2,1)} %bitcast.6), calls=%async_computation | async-start | bytes 4194304 | tf_op jit(solution)/shard_map/all_to_all | solution.py:16
  19.1 4.1 %multiply_reduce_fusion.1 = f32[]{:T(128)} fusion(f32[512,2048]{1,0:T(8,128)} %param.7), kind=kLoop, calls=%fused_computation.4 | loop fusion | flops 2097151 | bytes 4194308 | tf_op jit(solution)/shard_map/reduce_sum | solution.py:26
  23.3 77.5 %all-to-all-done = bf16[128,16,512]{0,2,1:T(8,128)(2,1)S(1)} async-done(((bf16[128,16,512]{0,2,1:T(8,128)(2,1)}), bf16[128,16,512]{0,2,1:T(8,128)(2,1)S(1)}, u32[]{:S(2)}, u32[]{:S(2)}) %all-to-all-start) | async-done | bytes 2097184 | tf_op jit(solution)/shard_map/all_to_all | solution.py:16
  100.7 2.6 copy.10
  103.3 52.0 %all-gather.2.cloned.1.call-done = bf16[2048,2048]{1,0:T(8,128)(2,1)} async-done(((bf16[128,2048]{1,0:T(8,128)(2,1)}), bf16[2048,2048]{1,0:T(8,128)(2,1)}) %all-gather.2.cloned.1.call-update) | async-done | bytes 8388624 | tf_op jit(solution)/shard_map/all_gather | solution.py:19
  155.4 0.0 copy-start.2
  155.4 0.0 copy-start.3
  155.4 10.9 %fusion.1 = (f32[512]{0:T(512)S(1)}, f32[2048]{0:T(1024)S(1)}, f32[512,2048]{1,0:T(8,128)}) fusion(bf16[2048,512]{1,0:T(8,128)(2,1)} %bitcast.7, bf16[2048,2048]{1,0:T(8,128)(2,1)} %all-gather.2.cloned.1.call-done), kind=kOutput, calls=%fused_computation.6 | convolution fusion | flops 4299159040 | bytes 14690304 | tf_op jit(solution)/shard_map/dot_general | solution.py:17
  166.3 30.4 %psum.30 = f32[2048]{0:T(1024)S(1)} all-reduce(f32[2048]{0:T(1024)S(1)} %get-tuple-element.5), channel_id=1, replica_groups=mesh['row'=16,'col'=2] {'row'}, use_global_device_ids=true, to_apply=%region_5.0 | all-reduce | flops 2048 | bytes 16384 | tf_op jit(solution)/shard_map/psum | solution.py:28
  196.7 2.5 psum.29
  199.2 0.0 copy-done.2
  199.2 0.0 copy-done.3
  199.2 0.0 copy-start
  199.2 0.0 copy-start.1
  199.2 4.1 %multiply_reduce_fusion = f32[]{:T(128)} fusion(f32[512,2048]{1,0:T(8,128)} %get-tuple-element.10, f32[2048]{0:T(1024)S(1)} %multiply_add_fusion.1, f32[512]{0:T(512)S(1)} %multiply_add_fusion.2), kind=kLoop, calls=%fused_computation.1 | loop fusion | flops 4194303 | bytes 4204548 | tf_op jit(solution)/shard_map/reduce_sum | solution.py:33
  203.3 49.3 %all-reduce = (f32[]{:T(128)}, f32[]{:T(128)}) all-reduce(f32[]{:T(128)} %multiply_reduce_fusion, f32[]{:T(128)} %multiply_reduce_fusion.1), channel_id=1, replica_groups=mesh['row'=16,'col'=2] {'row','col'}, use_global_device_ids=true, to_apply=%region_7.0 | all-reduce | flops 2 | bytes 16 | tf_op jit(solution)/shard_map/psum | solution.py:33
  253.9 8.9 %multiply_subtract_fusion = (f32[512,2048]{1,0:T(8,128)}, f32[512,2048]{1,0:T(8,128)}) fusion(f32[512,2048]{1,0:T(8,128)} %param.7, f32[]{:T(128)S(6)} %mul_shard_map.3, f32[]{:T(128)S(6)} %max_shard_map.3, f32[512,2048]{1,0:T(8,128)} %get-tuple-element.10, f32[2048]{0:T(1024)S(1)} %multiply_add_fusion.1, f32[512]{0:T(512)S(1)} %multiply_add_fusion.2), kind=kLoop, calls=%fused_computation | loop fusion | flops 5242880 | bytes 16787464 | tf_op jit(solution)/shard_map/sub | solution.py:38
  262.9 0.0 copy-done
  262.9 0.0 copy-done.1
  (2 shorter events, 0.0 us)
Async XLA Ops:
  7.2 148.2 %all-gather.2.cloned.1.call-start = ((), (), s32[]{:S(2)}) async-start(), calls=%async_computation.1 | async-start | bytes 8912896 | tf_op jit(solution)/shard_map/all_gather | solution.py:19
  12.0 88.8 %all-to-all-start = ((bf16[128,16,512]{0,2,1:T(8,128)(2,1)}), bf16[128,16,512]{0,2,1:T(8,128)(2,1)S(1)}, u32[]{:S(2)}, u32[]{:S(2)}) async-start(bf16[128,16,512]{0,2,1:T(8,128)(2,1)} %bitcast.6), calls=%async_computation | async-start | bytes 4194304 | tf_op jit(solution)/shard_map/all_to_all | solution.py:16
  155.4 43.8 %copy-start.2 = (f32[2048]{0:T(1024)S(1)}, f32[2048]{0:T(1024)}, u32[]{:S(2)}) copy-start(f32[2048]{0:T(1024)} %param.9) | copy-start | bytes 24580
  155.4 43.8 %copy-start.3 = (f32[512]{0:T(512)S(1)}, f32[512]{0:T(512)}, u32[]{:S(2)}) copy-start(f32[512]{0:T(512)} %param.8) | copy-start | bytes 6148
  199.2 63.7 %copy-start = (f32[2048]{0:T(1024)}, f32[2048]{0:T(1024)S(1)}, u32[]{:S(2)}) copy-start(f32[2048]{0:T(1024)S(1)} %multiply_add_fusion.1) | copy-start | bytes 24580
  199.2 63.6 %copy-start.1 = (f32[512]{0:T(512)}, f32[512]{0:T(512)S(1)}, u32[]{:S(2)}) copy-start(f32[512]{0:T(512)S(1)} %multiply_add_fusion.2) | copy-start | bytes 6148
Sparse Core Ops, SparseCore 0:
  10.7 144.5 all-gather.1
where the time goes:
time: 270 us
  waiting for transfers between devices  130 us (48%)
  blocking collectives  82.2 us (30%)
  other arithmetic  17.1 us (6%)
  between operations  15.4 us (6%)
  matrix products  10.9 us (4%)
  starting transfers between devices  7.21 us (3%)
  local copies, waits for them, and re-layouts  6.67 us (2%)
    all_to_all x1, waiting for transfers between devices, per_device(): lax.all_to_all(acts, 'row', split_axis=1, concat_axis=0, tiled=True)  77.5 us
    all_gather x1, waiting for transfers between devices, per_device(): lax.all_gather(out_grads, 'row', axis=0, tiled=True)  52 us
    psum x1, blocking collectives, per_device(): update_total = lax.psum(jnp.sum(unclipped * unclipped), ('row', 'col'))  49.3 us
    psum x1, blocking collectives, per_device(): col_total = lax.psum(col_squares, 'row')  30.4 us
    dot_general x1, matrix products, per_device(): lax.dot_general(columns, lax.all_gather(out_grads, 'row', axis=0, tiled=T...  10.9 us
    sub x1, other arithmetic, per_device(): new_weight = weight - step_size * update  8.93 us
    all_to_all x1, starting transfers between devices, per_device(): lax.all_to_all(acts, 'row', split_axis=1, concat_axis=0, tiled=True)  7.17 us
  transfers between devices with their start and end apart: 2, of which 2 were waited for; matrix products, arithmetic and copies ran while one was open for 4% of the time, Pallas kernels for 0%

commit v1 on v0

--- a/solution.py
+++ b/solution.py
@@ -8,15 +8,38 @@
 relative_rate = 0.05
 
 
+def keep_up_slot_here(tile_in, array_dim):
+    high = list(tile_in.shape[1:])
+    high[array_dim] *= tile_in.shape[0]
+    return jnp.moveaxis(tile_in, 0, array_dim).reshape(high)
+
+
+def _direct_surface(slab_in, comm_axis):
+    finding, z_new = (lax.axis_size(comm_axis), lax.axis_index(comm_axis))
+    res, h_now = (slab_in[None], 1)
+    while h_now < finding:
+        o_now = lax.ppermute(
+            res, axis_name=comm_axis, perm=list(map(lambda ii: (ii, ii ^ h_now), range(finding)))
+        )
+        new = z_new & h_now == 0
+        res = jnp.concatenate([jnp.where(new, res, o_now), jnp.where(new, o_now, res)])
+        h_now *= 2
+    return res
+
+
 def per_device(acts, out_grads, weight, row_state, col_state):
     n_col = lax.axis_size("col")
     width = acts.shape[1]
     cols_here = out_grads.shape[1]
     cols_all = cols_here * n_col
     columns = lax.all_to_all(acts, "row", split_axis=1, concat_axis=0, tiled=True)
+
+    def _feed_members_all(t0, target, k_dim):
+        return keep_up_slot_here(_direct_surface(t0, target), k_dim)
+
     gradient = lax.dot_general(
         columns,
-        lax.all_gather(out_grads, "row", axis=0, tiled=True),
+        _feed_members_all(out_grads, "row", 0),
         (((0,), (0,)), ((), ())),
         preferred_element_type=jnp.float32,
     )

time: 270 us -> 439 us (1.63)
  waiting for transfers between devices: 130 us -> 282 us
  local copies, waits for them, and re-layouts: 6.67 us -> 26.4 us
  between operations: 15.4 us -> 2.15 us
  other arithmetic: 17.1 us -> 24.8 us
    ppermute x0 -> x4, waiting for transfers between devices: none -> 264 us  [_direct_surface(): lax.ppermute(res, axis_name=comm_axis, perm=list(map(lambda ii: (ii, ii ^...]
    all_to_all x1, waiting for transfers between devices: 77.5 us -> 18 us  [per_device(): lax.all_to_all(acts, 'row', split_axis=1, concat_axis=0, tiled=True)]
    all_gather x1 -> x0, waiting for transfers between devices: 52 us -> none  [per_device(): lax.all_gather(out_grads, 'row', axis=0, tiled=True)]
    unnamed x9 -> x19, local copies, waits for them, and re-layouts: 4.09 us -> 22.4 us
    select_n x0 -> x4, other arithmetic: none -> 7.54 us  [_direct_surface(): jnp.where(new, res, o_now)]
    ppermute x0 -> x4, starting transfers between devices: none -> 5.23 us  [_direct_surface(): lax.ppermute(res, axis_name=comm_axis, perm=list(map(lambda ii: (ii, ii ^...]
  transfers between devices with their start and end apart: 2 -> 5, of which waited for: 2 -> 5; matrix products, arithmetic and copies ran while one was open for 4% -> 4% of each run, Pallas kernels for 0% -> 0%
where the time goes in v1:
time: 439 us
  waiting for transfers between devices  282 us (64%)
  blocking collectives  84.3 us (19%)
  local copies, waits for them, and re-layouts  26.4 us (6%)
  other arithmetic  24.8 us (6%)
  starting transfers between devices  10.4 us (2%)
  matrix products  8.94 us (2%)
    ppermute x4, waiting for transfers between devices, _direct_surface(): lax.ppermute(res, axis_name=comm_axis, perm=list(map(lambda ii: (ii, ii ^...  264 us
    psum x1, blocking collectives, per_device(): update_total = lax.psum(jnp.sum(unclipped * unclipped), ('row', 'col'))  49.4 us
    psum x1, blocking collectives, per_device(): col_total = lax.psum(col_squares, 'row')  32.4 us
    unnamed x19, local copies, waits for them, and re-layouts  22.4 us
    all_to_all x1, waiting for transfers between devices, per_device(): lax.all_to_all(acts, 'row', split_axis=1, concat_axis=0, tiled=True)  18 us
    dot_general x1, matrix products, per_device(): lax.dot_general(columns, _feed_members_all(out_grads, 'row', 0), (((0,),...  8.94 us
  transfers between devices with their start and end apart: 5, of which 5 were waited for; matrix products, arithmetic and copies ran while one was open for 4% of the time, Pallas kernels for 0%

profile of v1, /device:TPU:12, one launch (start us, length us, event | category | flops | bytes accessed | tf_op | source)
XLA Modules:
  0.0 438.6 jit_solution(15380795235197888577)
XLA Ops:
  0.6 1.3 copy.13
  1.9 1.6 collective-permute-start
  3.5 12.2 %collective-permute-done = bf16[1,128,2048]{1,2,0:T(8,128)(2,1)S(1)} collective-permute-done((bf16[1,128,2048]{1,2,0:T(8,128)(2,1)S(1)}, bf16[1,128,2048]{1,2,0:T(8,128)(2,1)S(1)}, u32[]{:S(2)}, u32[]{:S(2)}) %collective-permute-start) | collective-permute-done | bytes 524320 | tf_op jit(solution)/shard_map/ppermute | solution.py:21
  16.4 23.5 %collective-permute-done.1 = bf16[2,128,2048]{1,2,0:T(8,128)(2,1)S(1)} collective-permute-done((bf16[2,128,2048]{1,2,0:T(8,128)(2,1)S(1)}, bf16[2,128,2048]{1,2,0:T(8,128)(2,1)S(1)}, u32[]{:S(2)}, u32[]{:S(2)}) %collective-permute-start.1) | collective-permute-done | bytes 1048608 | tf_op jit(solution)/shard_map/ppermute | solution.py:21
  41.8 45.3 %collective-permute-done.2 = bf16[4,128,2048]{1,2,0:T(8,128)(2,1)} collective-permute-done((bf16[4,128,2048]{1,2,0:T(8,128)(2,1)S(1)}, bf16[4,128,2048]{1,2,0:T(8,128)(2,1)}, u32[]{:S(2)}, u32[]{:S(2)}) %collective-permute-start.2) | collective-permute-done | bytes 2097184 | tf_op jit(solution)/shard_map/ppermute | solution.py:21
  87.1 2.1 broadcast_select_fusion.3
  89.2 2.6 pad_maximum_fusion
  91.9 2.6 collective-permute-start.3
  94.5 4.1 copy.14
  98.5 3.9 copy.15
  102.5 5.1 %all-to-all-start = ((bf16[128,16,512]{2,0,1:T(8,128)(2,1)}), bf16[128,16,512]{2,0,1:T(8,128)(2,1)}, u32[]{:S(2)}, u32[]{:S(2)}) async-start(bf16[128,16,512]{2,0,1:T(8,128)(2,1)} %copy.15), calls=%async_computation | async-start | bytes 4194304 | tf_op jit(solution)/shard_map/all_to_all | solution.py:35
  107.6 4.1 multiply_reduce_fusion.1
  111.7 182.7 %collective-permute-done.3 = bf16[8,128,2048]{1,2,0:T(8,128)(2,1)} collective-permute-done((bf16[8,128,2048]{1,2,0:T(8,128)(2,1)}, bf16[8,128,2048]{1,2,0:T(8,128)(2,1)}, u32[]{:S(2)}, u32[]{:S(2)}) %collective-permute-start.3) | collective-permute-done | bytes 4194336 | tf_op jit(solution)/shard_map/ppermute | solution.py:21
  294.4 5.2 %broadcast_select_fusion.1 = (bf16[8,128,2048]{1,2,0:T(8,128)(2,1)}, bf16[8,128,2048]{1,2,0:T(8,128)(2,1)}) fusion(bf16[8,128,2048]{1,2,0:T(8,128)(2,1)} %collective-permute-done.3, pred[]{:T(512)S(6)} %eq.12, bf16[4,128,2048]{1,2,0:T(8,128)(2,1)S(1)} %copy-done.1, bf16[4,128,2048]{1,2,0:T(8,128)(2,1)S(1)} %get-tuple-element.20), kind=kLoop, calls=%fused_computation.12 | loop fusion | flops 6291456 | bytes 16777216 | tf_op jit(solution)/shard_map/jit(_where)/select_n | solution.py:25
  299.6 18.0 %all-to-all-done = bf16[128,16,512]{2,0,1:T(8,128)(2,1)} async-done(((bf16[128,16,512]{2,0,1:T(8,128)(2,1)}), bf16[128,16,512]{2,0,1:T(8,128)(2,1)}, u32[]{:S(2)}, u32[]{:S(2)}) %all-to-all-start) | async-done | bytes 2097184 | tf_op jit(solution)/shard_map/all_to_all | solution.py:35
  317.6 8.9 %fusion.6 = (f32[512]{0:T(512)S(1)}, f32[2048]{0:T(1024)S(1)}, f32[2048,512,1]{1,0,2:T(8,128)}) fusion(bf16[128,16,512]{2,0,1:T(8,128)(2,1)} %all-to-all-done, bf16[8,128,2048]{1,2,0:T(8,128)(2,1)} %get-tuple-element.19, bf16[8,128,2048]{1,2,0:T(8,128)(2,1)} %get-tuple-element.18), kind=kOutput, calls=%fused_computation.14 | convolution fusion | flops 4303353344 | bytes 14690304 | tf_op jit(solution)/shard_map/dot_general | solution.py:40
  326.5 32.4 %psum.30 = f32[2048]{0:T(1024)S(1)} all-reduce(f32[2048]{0:T(1024)S(1)} %get-tuple-element.13), channel_id=1, replica_groups=mesh['row'=16,'col'=2] {'row'}, use_global_device_ids=true, to_apply=%region_5.6 | all-reduce | flops 2048 | bytes 16384 | tf_op jit(solution)/shard_map/psum | solution.py:51
  358.9 2.5 psum.29
  361.4 4.2 multiply_reduce_fusion
  365.6 5.3 %copy.16 = f32[512,2048]{0,1:T(8,128)} copy(f32[512,2048]{1,0:T(8,128)} %param.7) | data formatting | bytes 8388608 | tf_op args[2]
  371.0 49.4 %all-reduce = (f32[]{:T(128)}, f32[]{:T(128)}) all-reduce(f32[]{:T(128)} %multiply_reduce_fusion, f32[]{:T(128)} %multiply_reduce_fusion.1), channel_id=1, replica_groups=mesh['row'=16,'col'=2] {'row','col'}, use_global_device_ids=true, to_apply=%region_7.8 | all-reduce | flops 2 | bytes 16 | tf_op jit(solution)/shard_map/psum | solution.py:56
  421.8 6.1 %multiply_subtract_fusion = (f32[512,2048]{0,1:T(8,128)}, f32[512,2048]{0,1:T(8,128)}) fusion(f32[512,2048]{0,1:T(8,128)} %copy.16, f32[]{:T(128)S(6)} %mul_shard_map.3, f32[]{:T(128)S(6)} %max_shard_map.3, f32[2048]{0:T(1024)S(1)} %multiply_add_fusion, f32[512]{0:T(512)S(1)} %multiply_add_fusion.1, f32[2048,512,1]{1,0,2:T(8,128)} %get-tuple-element.26), kind=kLoop, calls=%fused_computation.8 | loop fusion | flops 5242880 | bytes 16787464 | tf_op jit(solution)/shard_map/sub | solution.py:61
  427.9 5.3 %copy.17 = f32[512,2048]{1,0:T(8,128)} copy(f32[512,2048]{0,1:T(8,128)} %get-tuple-element.16) | data formatting | bytes 8388608
  433.2 5.3 %copy.18 = f32[512,2048]{1,0:T(8,128)} copy(f32[512,2048]{0,1:T(8,128)} %get-tuple-element.17) | data formatting | bytes 8388608
  (22 shorter events, 2.6 us)
Async XLA Ops:
  1.9 13.7 %collective-permute-start = (bf16[1,128,2048]{1,2,0:T(8,128)(2,1)S(1)}, bf16[1,128,2048]{1,2,0:T(8,128)(2,1)S(1)}, u32[]{:S(2)}, u32[]{:S(2)}) collective-permute-start(bf16[1,128,2048]{1,2,0:T(8,128)(2,1)S(1)} %bitcast.26), channel_id=1, source_target_pairs={{0,2},{2,0},{4,6},{6,4},{8,10},{10,8},{12,14},{14,12},{16,18},{18,... | collective-permute-start | bytes 1572872 | tf_op jit(solution)/shard_map/ppermute | solution.py:21
  15.9 24.1 %collective-permute-start.1 = (bf16[2,128,2048]{1,2,0:T(8,128)(2,1)S(1)}, bf16[2,128,2048]{1,2,0:T(8,128)(2,1)S(1)}, u32[]{:S(2)}, u32[]{:S(2)}) collective-permute-start(bf16[2,128,2048]{1,2,0:T(8,128)(2,1)S(1)} %pad_maximum_fusion.2), channel_id=1, source_target_pairs={{0,4},{2,6},{4,0},{6,2},{8,12},{10,14},{12,8},{14,10},{16,20},{18,... | collective-permute-start | bytes 3145736 | tf_op jit(solution)/shard_map/ppermute | solution.py:21
  40.1 1.0 copy-start.2
  41.3 45.8 %collective-permute-start.2 = (bf16[4,128,2048]{1,2,0:T(8,128)(2,1)S(1)}, bf16[4,128,2048]{1,2,0:T(8,128)(2,1)}, u32[]{:S(2)}, u32[]{:S(2)}) collective-permute-start(bf16[4,128,2048]{1,2,0:T(8,128)(2,1)S(1)} %pad_maximum_fusion.1), channel_id=1, source_target_pairs={{0,8},{2,10},{4,12},{6,14},{8,0},{10,2},{12,4},{14,6},{16,24},{18,... | collective-permute-start | bytes 6291464 | tf_op jit(solution)/shard_map/ppermute | solution.py:21
  89.2 2.7 copy-start
  91.9 202.5 %collective-permute-start.3 = (bf16[8,128,2048]{1,2,0:T(8,128)(2,1)}, bf16[8,128,2048]{1,2,0:T(8,128)(2,1)}, u32[]{:S(2)}, u32[]{:S(2)}) collective-permute-start(bf16[8,128,2048]{1,2,0:T(8,128)(2,1)} %pad_maximum_fusion), channel_id=1, source_target_pairs={{0,16},{2,18},{4,20},{6,22},{8,24},{10,26},{12,28},{14,30},{16,0},... | collective-permute-start | bytes 12582920 | tf_op jit(solution)/shard_map/ppermute | solution.py:21
  102.5 215.1 %all-to-all-start = ((bf16[128,16,512]{2,0,1:T(8,128)(2,1)}), bf16[128,16,512]{2,0,1:T(8,128)(2,1)}, u32[]{:S(2)}, u32[]{:S(2)}) async-start(bf16[128,16,512]{2,0,1:T(8,128)(2,1)} %copy.15), calls=%async_computation | async-start | bytes 4194304 | tf_op jit(solution)/shard_map/all_to_all | solution.py:35
  107.6 186.8 %copy-start.1 = (bf16[4,128,2048]{1,2,0:T(8,128)(2,1)S(1)}, bf16[4,128,2048]{1,2,0:T(8,128)(2,1)}, u32[]{:S(2)}) copy-start(bf16[4,128,2048]{1,2,0:T(8,128)(2,1)} %copy-done) | copy-start | bytes 6291460
  317.6 43.8 %copy-start.5 = (f32[2048]{0:T(1024)S(1)}, f32[2048]{0:T(1024)}, u32[]{:S(2)}) copy-start(f32[2048]{0:T(1024)} %param.9) | copy-start | bytes 24580
  317.6 43.8 %copy-start.6 = (f32[512]{0:T(512)S(1)}, f32[512]{0:T(512)}, u32[]{:S(2)}) copy-start(f32[512]{0:T(512)} %param.8) | copy-start | bytes 6148
  361.4 60.4 %copy-start.3 = (f32[2048]{0:T(1024)}, f32[2048]{0:T(1024)S(1)}, u32[]{:S(2)}) copy-start(f32[2048]{0:T(1024)S(1)} %multiply_add_fusion) | copy-start | bytes 24580
  361.4 60.4 %copy-start.4 = (f32[512]{0:T(512)}, f32[512]{0:T(512)S(1)}, u32[]{:S(2)}) copy-start(f32[512]{0:T(512)S(1)} %multiply_add_fusion.1) | copy-start | bytes 6148
